TPU v7x, 512 devices: a whole 4x8x8 slice. The times are simulated.
512 devices in a mesh: seq: 32 (over z_hi, y), dp: 16 (over z_lo, x, core).
Axes of the slice: x: 4, y: 8, z: 8 (z_hi: 4, z_lo: 2; z = z_hi * 2 + z_lo), core: 2. Of those that a mesh axis runs over, the one named last changes fastest.
Arguments:
- queries: bfloat16 [16, 4096, 1024], P('dp', 'seq'), may hold values from -150 to 150
- key_states: bfloat16 [16, 4096, 1024], P('dp', 'seq'), may hold values from -6 to 6
- values: bfloat16 [16, 4096, 1024], P('dp', 'seq'), may hold values from -6 to 6
- w_out: bfloat16 [1024, 1024], replicated, may hold values from -0.1875 to 0.1875
- cotangent: bfloat16 [16, 4096, 1024], P('dp', 'seq'), may hold values from -6 to 6
- neighbours: int32 [16, 32, 2], P('dp', 'seq'), may hold values from 0 to 31, as said below
- counts: int32 [16, 32], P('dp', 'seq'), may hold values from 1 to 2
Outputs:
- output: bfloat16 [16, 4096, 1024], P('dp', 'seq')
- grad_queries: bfloat16 [16, 4096, 1024], P('dp', 'seq')
- grad_keys: bfloat16 [16, 4096, 1024], P('dp', 'seq')
- grad_values: bfloat16 [16, 4096, 1024], P('dp', 'seq')
- grad_w_out: float32 [1024, 1024], P(('seq', 'dp'))
Inputs may be any that keep to these rules, and one draw needn't show every extreme that they name: `neighbours`: entries j < counts[s, p] of patch p's list are distinct patches other than p, at most 1 patches away from p; the later entries equal p.
All inputs are finite; a program needn't handle non-finite values.
Results may differ from a plain program's by a relative error of at most 0.029.
Values may be sent and summed in bfloat16 or wider, within the bound.
A program may use at most 64 MiB of HBM per device.

v0:
```python
import math

import jax
import jax.numpy as jnp
from jax import lax
from jax.sharding import PartitionSpec as P

HD = 128
REACH = 1


def passed_along(value, axis, by):
    count = lax.axis_size(axis)
    pairs = [(i, i + by) for i in range(count) if 0 <= i + by < count]
    return lax.ppermute(value, axis, pairs)


def fetch_patch(key_value, offset):
    return passed_along(key_value, "seq", -offset)


def return_parts(outgoing, offset):
    return passed_along(outgoing, "seq", offset)


def attend(query_rows, key_block, value_block, allowed, w_out, cot_rows):
    score_scale = 1.0 / math.sqrt(HD)
    patch_rows = query_rows.shape[0]
    feature_count = query_rows.shape[1]
    head_count = feature_count // HD
    query_heads = query_rows.reshape(patch_rows, head_count, HD)
    key_heads = key_block.reshape(-1, head_count, HD)
    value_heads = value_block.reshape(-1, head_count, HD)
    scores = (
        jnp.einsum("qhd,khd->hqk", query_heads, key_heads, preferred_element_type=jnp.float32)
        * score_scale
    )
    scores = jnp.where(allowed[None, None, :], scores, -jnp.inf)
    row_max = jnp.max(scores, axis=-1, keepdims=True)
    log_total = row_max + jnp.log(jnp.sum(jnp.exp(scores - row_max), axis=-1, keepdims=True))
    attn_probs = jnp.exp(scores - log_total)
    probs_low = attn_probs.astype(jnp.bfloat16)
    attended = jnp.einsum(
        "hqk,khd->qhd", probs_low, value_heads, preferred_element_type=jnp.float32
    )
    attended = attended.reshape(patch_rows, feature_count).astype(jnp.bfloat16)
    output = jnp.dot(attended, w_out, preferred_element_type=jnp.float32).astype(jnp.bfloat16)
    grad_attended = lax.dot_general(
        cot_rows, w_out, (((1,), (1,)), ((), ())), preferred_element_type=jnp.float32
    ).astype(jnp.bfloat16)
    grad_heads = grad_attended.reshape(patch_rows, head_count, HD)
    attn_heads = attended.reshape(patch_rows, head_count, HD)
    row_delta = jnp.sum(grad_heads.astype(jnp.float32) * attn_heads.astype(jnp.float32), axis=-1).T[
        :, :, None
    ]
    grad_probs = jnp.einsum(
        "qhd,khd->hqk", grad_heads, value_heads, preferred_element_type=jnp.float32
    )
    grad_scores = (attn_probs * (grad_probs - row_delta)).astype(jnp.bfloat16)
    grad_query = (
        jnp.einsum("hqk,khd->qhd", grad_scores, key_heads, preferred_element_type=jnp.float32)
        * score_scale
    )
    grad_query = grad_query.reshape(patch_rows, feature_count).astype(jnp.bfloat16)
    key_parts = (
        jnp.einsum("hqk,qhd->khd", grad_scores, query_heads, preferred_element_type=jnp.float32)
        * score_scale
    )
    key_parts = key_parts.reshape(-1, patch_rows, feature_count).astype(jnp.bfloat16)
    value_parts = jnp.einsum(
        "hqk,qhd->khd", probs_low, grad_heads, preferred_element_type=jnp.float32
    )
    value_parts = value_parts.reshape(-1, patch_rows, feature_count).astype(jnp.bfloat16)
    return (output, grad_query, key_parts, value_parts, attended)


def on_device(queries, key_states, values, w_out, cotangent, neighbours, counts):
    query_rows = queries[0]
    cot_rows = cotangent[0]
    listed = neighbours[0, 0]
    live_count = counts[0, 0]
    patch_rows = query_rows.shape[0]
    feature_count = query_rows.shape[1]
    patch_id = lax.axis_index("seq")
    key_value = jnp.stack([key_states[0], values[0]])
    gathered = []
    for offset in range(-REACH, REACH + 1):
        gathered.append(key_value if offset == 0 else fetch_patch(key_value, offset))
    window = jnp.stack(gathered)
    offsets = jnp.arange(-REACH, REACH + 1, dtype=jnp.int32)
    slot_ids = jnp.arange(listed.shape[0], dtype=jnp.int32)
    matches = (listed[None, :] == patch_id + offsets[:, None]) & (slot_ids[None, :] < live_count)
    window_flags = jnp.any(matches, axis=1) | (offsets == 0)
    chosen = offsets + REACH
    key_block = window[:, 0].reshape(-1, feature_count)
    value_block = window[:, 1].reshape(-1, feature_count)
    allowed = jnp.repeat(window_flags, patch_rows)
    output, grad_query, key_parts, value_parts, attended = attend(
        query_rows, key_block, value_block, allowed, w_out, cot_rows
    )
    parts = jnp.stack([key_parts, value_parts], axis=1)
    summed = jnp.zeros((2, patch_rows, feature_count), jnp.float32)
    for position, offset in enumerate(range(-REACH, REACH + 1)):
        selected = (chosen == position) & window_flags
        outgoing = jnp.sum(
            jnp.where(selected[:, None, None, None], parts, jnp.zeros_like(parts)), axis=0
        )
        if offset == 0:
            summed = summed + outgoing.astype(jnp.float32)
        else:
            summed = summed + return_parts(outgoing, offset).astype(jnp.float32)
    grad_key = summed[0].astype(jnp.bfloat16)
    grad_value = summed[1].astype(jnp.bfloat16)
    term = lax.dot_general(
        attended, cot_rows, (((0,), (0,)), ((), ())), preferred_element_type=jnp.float32
    )
    seq_part = lax.psum_scatter(
        lax.optimization_barrier(term.astype(jnp.bfloat16))
        .astype(jnp.float32)
        .astype(jnp.bfloat16),
        "seq",
        scatter_dimension=0,
        tiled=True,
    )
    grad_weight = lax.psum_scatter(seq_part, "dp", scatter_dimension=0, tiled=True).astype(
        jnp.float32
    )
    return (output[None], grad_query[None], grad_key[None], grad_value[None], grad_weight)


def solution(mesh):
    placed = (
        P("dp", "seq", None),
        P("dp", "seq", None),
        P("dp", "seq", None),
        P(),
        P("dp", "seq", None),
        P("dp", "seq", None),
        P("dp", "seq"),
    )
    return jax.shard_map(
        on_device,
        mesh=mesh,
        in_specs=placed,
        out_specs=(
            P("dp", "seq", None),
            P("dp", "seq", None),
            P("dp", "seq", None),
            P("dp", "seq", None),
            P(("seq", "dp"), None),
        ),
        check_vma=False,
    )
```

profile of v0, /device:TPU:6, one launch (start us, length us, event | category | flops | bytes accessed | tf_op | source)
XLA Modules:
  0.0 421.1 jit_solution(623099782719419725)
XLA Ops:
  9.3 1.3 collective-permute-start.1
  10.6 5.3 %collective-permute-start = (bf16[2,128,1024]{2,1,0:T(8,128)(2,1)S(1)}, bf16[2,128,1024]{2,1,0:T(8,128)(2,1)}, u32[]{:S(2)}, u32[]{:S(2)}) collective-permute-start(bf16[2,128,1024]{2,1,0:T(8,128)(2,1)S(1)} %constant_dynamic-update-slice_fusion), channel_id=1, source_target_pairs={{0,16},{16,32},{32,48},{48,64},{64,80},{80,96},{96,112},{112,128},... | collective-permute-start | bytes 1572872 | tf_op jit(solution)/shard_map/ppermute | solution.py:15
  17.7 1.5 convolution_convert_fusion.2
  20.6 4.4 %collective-permute-done.1 = bf16[2,128,1024]{2,1,0:T(8,128)(2,1)} collective-permute-done((bf16[2,128,1024]{2,1,0:T(8,128)(2,1)S(1)}, bf16[2,128,1024]{2,1,0:T(8,128)(2,1)}, u32[]{:S(2)}, u32[]{:S(2)}) %collective-permute-start.1) | collective-permute-done | bytes 524320 | tf_op jit(solution)/shard_map/ppermute | solution.py:15
  26.1 1.4 pad_maximum_fusion
  29.6 1.6 copy.62
  31.2 1.3 copy.74
  34.9 2.0 convolution_convert_fusion
  37.0 2.1 multiply_convert_fusion.1
  40.3 1.4 copy.65
  41.8 2.2 convert_element_type.119
  43.9 2.8 fusion.4
  46.7 2.5 copy.67
  49.2 2.1 convert_element_type.122
  52.8 2.2 select_reduce_fusion.2
  54.9 1.4 collective-permute-start.2
  56.4 5.9 %collective-permute-start.3 = (bf16[2,128,1024]{2,1,0:T(8,128)(2,1)}, bf16[2,128,1024]{2,1,0:T(8,128)(2,1)}, u32[]{:S(2)}, u32[]{:S(2)}) collective-permute-start(bf16[2,128,1024]{2,1,0:T(8,128)(2,1)} %get-tuple-element.26), channel_id=1, source_target_pairs={{0,16},{16,32},{32,48},{48,64},{64,80},{80,96},{96,112},{112,128},... | collective-permute-start | bytes 1572872 | tf_op jit(solution)/shard_map/ppermute | solution.py:15
  64.2 1.5 fusion.6
  67.8 2.8 collective-permute-done.2
  70.6 1.5 collective-permute-done.3
  72.1 1.5 add_convert_fusion
  73.6 225.1 %reduce-scatter.2.cloned.1.call-done = bf16[32,1024]{1,0:T(8,128)(2,1)} async-done(((bf16[1024,1024]{1,0:T(8,128)(2,1)}), bf16[32,1024]{1,0:T(8,128)(2,1)}) %reduce-scatter.2.cloned.1.call-update) | async-done | bytes 65552 | tf_op jit(solution)/shard_map/reduce_scatter | solution.py:117
  299.5 113.4 %all-reduce.3.cloned.1.call-done = bf16[32,1024]{1,0:T(8,128)(2,1)} async-done(((bf16[32,1024]{1,0:T(8,128)(2,1)}), bf16[32,1024]{1,0:T(8,128)(2,1)}) %all-reduce.3.cloned.1.call-update) | async-done | bytes 65552
  413.0 1.3 dynamic-slice_convert_fusion
  (50 shorter events, 16.9 us)
Async XLA Ops:
  7.2 10.5 %copy-start = (bf16[1024,1024]{1,0:T(8,128)(2,1)S(1)}, bf16[1024,1024]{1,0:T(8,128)(2,1)}, u32[]{:S(2)}) copy-start(bf16[1024,1024]{1,0:T(8,128)(2,1)} %param.10) | copy-start | bytes 6291460
  7.2 10.5 %copy-start.8 = (bf16[1,128,1024]{2,1,0:T(8,128)(2,1)S(1)}, bf16[1,128,1024]{2,1,0:T(8,128)(2,1)}, u32[]{:S(2)}) copy-start(bf16[1,128,1024]{2,1,0:T(8,128)(2,1)} %param.11) | copy-start | bytes 786436
  7.2 291.5 %reduce-scatter.2.cloned.1.call-start = ((), (), s32[]{:S(2)}) async-start(), calls=%async_computation.1 | async-start | bytes 2162688 | tf_op jit(solution)/shard_map/reduce_scatter | solution.py:117
  9.3 15.7 %collective-permute-start.1 = (bf16[2,128,1024]{2,1,0:T(8,128)(2,1)S(1)}, bf16[2,128,1024]{2,1,0:T(8,128)(2,1)}, u32[]{:S(2)}, u32[]{:S(2)}) collective-permute-start(bf16[2,128,1024]{2,1,0:T(8,128)(2,1)S(1)} %constant_dynamic-update-slice_fusion), channel_id=1, source_target_pairs={{16,0},{32,16},{48,32},{64,48},{80,64},{96,80},{112,96},{128,112},... | collective-permute-start | bytes 1572872 | tf_op jit(solution)/shard_map/ppermute | solution.py:15
  10.6 15.4 %collective-permute-start = (bf16[2,128,1024]{2,1,0:T(8,128)(2,1)S(1)}, bf16[2,128,1024]{2,1,0:T(8,128)(2,1)}, u32[]{:S(2)}, u32[]{:S(2)}) collective-permute-start(bf16[2,128,1024]{2,1,0:T(8,128)(2,1)S(1)} %constant_dynamic-update-slice_fusion), channel_id=1, source_target_pairs={{0,16},{16,32},{32,48},{48,64},{64,80},{80,96},{96,112},{112,128},... | collective-permute-start | bytes 1572872 | tf_op jit(solution)/shard_map/ppermute | solution.py:15
  17.7 2.7 copy-start.10
  32.5 0.9 copy-start.3
  33.0 1.1 copy-start.1
  33.2 1.6 copy-start.9
  34.1 0.7 copy-start.5
  36.9 376.1 %all-reduce.3.cloned.1.call-start = ((), (), s32[]{:S(2)}) async-start(), calls=%async_computation.2 | async-start | bytes 131072
  39.1 0.9 copy-start.2
  51.4 1.4 copy-start.4
  54.9 11.6 %copy-start.6 = (bf16[8,128,128]{2,1,0:T(8,128)(2,1)S(1)}, bf16[8,128,128]{2,1,0:T(8,128)(2,1)}, u32[]{:S(2)}) copy-start(bf16[8,128,128]{2,1,0:T(8,128)(2,1)} %copy-done.5) | copy-start | bytes 786436
  54.9 15.7 %collective-permute-start.2 = (bf16[2,128,1024]{2,1,0:T(8,128)(2,1)}, bf16[2,128,1024]{2,1,0:T(8,128)(2,1)}, u32[]{:S(2)}, u32[]{:S(2)}) collective-permute-start(bf16[2,128,1024]{2,1,0:T(8,128)(2,1)} %get-tuple-element.25), channel_id=1, source_target_pairs={{16,0},{32,16},{48,32},{64,48},{80,64},{96,80},{112,96},{128,112},... | collective-permute-start | bytes 1572872 | tf_op jit(solution)/shard_map/ppermute | solution.py:15
  56.4 15.8 %collective-permute-start.3 = (bf16[2,128,1024]{2,1,0:T(8,128)(2,1)}, bf16[2,128,1024]{2,1,0:T(8,128)(2,1)}, u32[]{:S(2)}, u32[]{:S(2)}) collective-permute-start(bf16[2,128,1024]{2,1,0:T(8,128)(2,1)} %get-tuple-element.26), channel_id=1, source_target_pairs={{0,16},{16,32},{32,48},{48,64},{64,80},{80,96},{96,112},{112,128},... | collective-permute-start | bytes 1572872 | tf_op jit(solution)/shard_map/ppermute | solution.py:15
  65.7 6.4 %copy-start.7 = (bf16[2,128,1024]{2,1,0:T(8,128)(2,1)S(1)}, bf16[2,128,1024]{2,1,0:T(8,128)(2,1)}, u32[]{:S(2)}) copy-start(bf16[2,128,1024]{2,1,0:T(8,128)(2,1)} %get-tuple-element.27) | copy-start | bytes 1572868
Sparse Core Ops, SparseCore 0:
  37.0 261.6 reduce-scatter.1
  301.9 111.0 all-reduce.2
where the time goes:
time: 425 us; the launch traced here: 421 us
  waiting for transfers between devices  348 us (82%)
  local copies, waits for them, and re-layouts  23.8 us (6%)
  between operations  15.6 us (4%)
  starting transfers between devices  14.1 us (3%)
  matrix products  12.6 us (3%)
  other arithmetic  6.76 us (2%)
    reduce_scatter x1, waiting for transfers between devices, on_device(): lax.psum_scatter(lax.optimization_barrier(term.astype(jnp.bfloat16)).asty...  225 us
    unnamed x3, waiting for transfers between devices  113 us
    ppermute x4, starting transfers between devices, passed_along(): return lax.ppermute(value, axis, pairs)  14 us
    unnamed x29, local copies, waits for them, and re-layouts  9.92 us
    ppermute x4, waiting for transfers between devices, passed_along(): return lax.ppermute(value, axis, pairs)  9.82 us
  transfers between devices with their start and end apart: 6, of which 6 were waited for; matrix products, arithmetic and copies ran while one was open for 7% of the time, Pallas kernels for 0%

commit v1 on v0

v1 whole, which is shorter than its diff:
```python
import functools
import math

import jax
import jax.numpy as jnp
from jax import lax
from jax.experimental import pallas as pl
from jax.experimental.pallas import tpu as pltpu
from jax.sharding import PartitionSpec as P

HD = 128
PAIRS = 4
PW = 2 * HD
BF = jnp.bfloat16
F32 = jnp.float32
NX, NY, NZ = 4, 8, 8
MESH = pl.DeviceIdType.MESH


def dot(a, b, ca, cb):
    return lax.dot_general(a, b, (((ca,), (cb,)), ((), ())), preferred_element_type=F32)


def kernel(
    nbr, cnt, q_h, k_h, v_h, w_h, c_h,
    out_h, dq_h, dk_h, dv_h, gw_h,
    q, kv, w, cot, do, att, dq, kvp, kvr, asend, aall, zs, zr, ys, yr, outv, gkv, gw,
    lq, lkv, lw, lc, lo,
    hs, hr, cs, cr, as_, ar, ps, pr_, zss, zrs, yss, yrs,
):
    s = lax.axis_index("seq")
    d = lax.axis_index("dp")
    z_hi, y = s // NY, s % NY
    z_lo, xc = d // 8, d % 8
    x, core = xc // 2, xc % 2
    z = z_hi * 2 + z_lo
    right, left = (s + 1) % 32, (s + 31) % 32

    def dev(ss, dd):
        return {"seq": ss, "dp": dd}

    def grp(j):
        return dev(s, z_lo * 8 + j)

    def zdev(zz):
        return dev((zz // 2) * NY + y, (zz % 2) * 8 + xc)

    def ydev(yy):
        return dev(z_hi * NY + yy, d)

    loads = {}

    def load(key, src, dst, sem):
        c = pltpu.make_async_copy(src, dst, sem)
        c.start()
        loads[key] = c

    for i in range(PAIRS):
        cols = pl.ds(i * PW, PW)
        load(("k", i), k_h.at[0, :, cols], kv.at[i, 0, pl.ds(128, 128), :], lkv.at[i, 0])
        load(("v", i), v_h.at[0, :, cols], kv.at[i, 1, pl.ds(128, 128), :], lkv.at[i, 1])
    load("c", c_h.at[0], cot.at[xc], lc)
    for i in range(PAIRS):
        load(("w", i), w_h.at[pl.ds(i * PW, PW), :], w.at[i], lw.at[i])
        load(("q", i), q_h.at[0, :, pl.ds(i * PW, PW)], q.at[i], lq.at[i])

    barrier = pltpu.get_barrier_semaphore()
    peers = [dev(right, d), dev(left, d)]
    peers += [grp((xc + k) % 8) for k in range(1, 8)]
    peers += [zdev((z + k) % NZ) for k in range(1, NZ)]
    peers += [ydev((y + k) % NY) for k in range(1, NY)]
    for peer in peers:
        pl.semaphore_signal(barrier, inc=1, device_id=peer, device_id_type=MESH)
    pl.semaphore_wait(barrier, len(peers))

    sends = []

    def remote(src, dst, ss, rs, to):
        return pltpu.make_async_remote_copy(
            src_ref=src, dst_ref=dst, send_sem=ss, recv_sem=rs, device_id=to, device_id_type=MESH
        )

    def send(*args):
        c = remote(*args)
        c.start()
        sends.append(c)

    mid = pl.ds(128, 128)
    lo_rows = pl.ds(0, 128)
    hi_rows = pl.ds(256, 128)
    xr = ((x + 1) % NX) * 2 + core
    xl = ((x + 3) % NX) * 2 + core
    xo = ((x + 2) % NX) * 2 + core
    partner = x * 2 + (1 - core)
    half = (pl.ds(0, 64), pl.ds(64, 64))

    def halo(i, way):
        if way == 0:
            return remote(kv.at[i, :, mid, :], kv.at[i, :, lo_rows, :], hs.at[0, i], hr.at[0, i], dev(right, d))
        return remote(kv.at[i, :, mid, :], kv.at[i, :, hi_rows, :], hs.at[1, i], hr.at[1, i], dev(left, d))

    for i in range(PAIRS):
        loads["k", i].wait()
        loads["v", i].wait()
        for way in range(2):
            c = halo(i, way)
            c.start()
            sends.append(c)
        if i == 0:
            loads["c"].wait()
            mine = cot.at[xc]
            for n, (to, first) in enumerate(((xr, 0), (xl, 1))):
                for m, hh in enumerate((first, 1 - first)):
                    send(mine.at[half[hh], :], mine.at[half[hh], :], cs.at[n, m], cr.at[n, m], grp(to))
            send(mine, mine, cs.at[2, 0], cr.at[2, 0], grp(partner))

    c_own = cot[xc]
    for i in range(PAIRS):
        loads["w", i].wait()
        do[i] = dot(c_own, w[i], 1, 1).astype(BF)
    for i in range(PAIRS):
        loads["q", i].wait()

    n0, n1, live = nbr[0, 0, 0], nbr[0, 0, 1], cnt[0, 0]
    neg = -jnp.inf

    def bias(target):
        hit = ((n0 == target) & (live > 0)) | ((n1 == target) & (live > 1))
        return jnp.where(hit, 0.0, neg).astype(F32)

    b_left, b_right = bias(s - 1), bias(s + 1)
    scale = 1.0 / math.sqrt(HD)

    o_id = lax.broadcasted_iota(jnp.int32, (PW, PW), 0)
    f_id = lax.broadcasted_iota(jnp.int32, (PW, PW), 1)
    f_of = ((o_id >> 1) & 7) * 32 + ((o_id >> 4) & 1) * 16 + ((o_id >> 5) & 7) * 2 + (o_id & 1)
    perm = jnp.where(f_id == f_of, 1.0, 0.0).astype(BF)

    def cot_wait(slot, rows, n, m):
        ref = cot.at[slot] if rows is None else cot.at[slot].at[half[rows], :]
        remote(ref, ref, cs.at[n, m], cr.at[n, m], grp(partner)).wait_recv()

    for i in range(PAIRS):
        for way in range(2):
            halo(i, way).wait_recv()
        for h in range(2):
            cols = pl.ds(h * HD, HD)
            qh, doh = q[i, :, cols], do[i, :, cols]
            kh, vh = kv[i, 0, :, cols], kv[i, 1, :, cols]
            t = dot(kh, qh, 1, 1) * scale
            t = jnp.concatenate([t[:128] + b_left, t[128:256], t[256:] + b_right], axis=0)
            e = jnp.exp(t - jnp.max(t, axis=0, keepdims=True))
            p = e * (1.0 / jnp.sum(e, axis=0, keepdims=True))
            pb = p.astype(BF)
            att_h = dot(pb, vh, 0, 0).astype(BF)
            att[:, pl.ds(i * PW + h * HD, HD)] = att_h
            dp = dot(vh, doh, 1, 1)
            delta = jnp.sum(p * dp, axis=0, keepdims=True)
            ds = (p * (dp - delta)).astype(BF)
            dq[i, :, cols] = (dot(ds, kh, 0, 0) * scale).astype(BF)
            kvp[i, 0, :, cols] = (dot(ds, qh, 1, 0) * scale).astype(BF)
            kvp[i, 1, :, cols] = dot(pb, doh, 1, 0).astype(BF)
        a_pair = att[:, pl.ds(i * PW, PW)]
        asend[i] = dot(perm, a_pair, 1, 1).astype(BF).reshape(8, 32, 128)
        rows = pl.ds(i * 32, 32)
        for k in range(1, 8):
            j = (xc + k) % 8
            send(asend.at[i, j], aall.at[xc, rows, :], as_.at[i, k], ar.at[i, k], grp(j))
        aall[xc, rows, :] = asend[i, xc]
        send(kvp.at[i, :, hi_rows, :], kvr.at[0, i], ps.at[0, i], pr_.at[0, i], dev(right, d))
        send(kvp.at[i, :, lo_rows, :], kvr.at[1, i], ps.at[1, i], pr_.at[1, i], dev(left, d))
        if i == 0:
            cot_wait(xl, 0, 0, 0)
            ref = cot.at[xl].at[half[0], :]
            send(ref, ref, cs.at[3, 0], cr.at[3, 0], grp(xr))
            cot_wait(xr, 1, 1, 0)
            ref = cot.at[xr].at[half[1], :]
            send(ref, ref, cs.at[3, 1], cr.at[3, 1], grp(xl))
        if i == 2:
            cot_wait(xl, 1, 0, 1)
            send(cot.at[xl], cot.at[xl], cs.at[4, 0], cr.at[4, 0], grp(partner))
            cot_wait(xr, 0, 1, 1)
            send(cot.at[xr], cot.at[xr], cs.at[4, 1], cr.at[4, 1], grp(partner))
            cot_wait(xo, 0, 3, 0)
            cot_wait(xo, 1, 3, 1)
            send(cot.at[xo], cot.at[xo], cs.at[2, 1], cr.at[2, 1], grp(partner))

    outs = []

    def store(src, dst, sem):
        c = pltpu.make_async_copy(src, dst, sem)
        c.start()
        outs.append(c)

    for i in range(PAIRS):
        store(dq.at[i], dq_h.at[0, :, pl.ds(i * PW, PW)], lo.at[i])
    a_all = att[...]
    outv[...] = sum(dot(a_all[:, i * PW:(i + 1) * PW], w[i], 1, 0) for i in range(PAIRS)).astype(BF)
    store(outv, out_h.at[0], lo.at[4])

    def flip(slot):
        return (slot // 2) * 2 + (1 - slot % 2)

    cot_wait(partner, None, 2, 0)
    cot_wait(flip(xl), None, 4, 0)
    cot_wait(flip(xr), None, 4, 1)
    cot_wait(flip(xo), None, 2, 1)
    for i in range(PAIRS):
        for k in range(1, 8):
            j = (xc + 8 - k) % 8
            ref = aall.at[j, pl.ds(i * 32, 32), :]
            remote(ref, ref, as_.at[i, k], ar.at[i, k], grp(j)).wait_recv()
    a_t = jnp.concatenate([aall[j] for j in range(8)], axis=1)
    zs[...] = dot(a_t, cot[...].reshape(1024, 1024), 1, 0).astype(BF).reshape(NZ, 16, 1024)
    for k in range(1, NZ):
        zz = (z + k) % NZ
        send(zs.at[zz], zr.at[k], zss.at[k], zrs.at[k], zdev(zz))
    total = zs[z].astype(F32)
    for k in range(1, NZ):
        remote(zr.at[k], zr.at[k], zss.at[k], zrs.at[k], zdev((z + NZ - k) % NZ)).wait_recv()
        total = total + zr[k].astype(F32)
    for j in range(NY):
        ys[j] = total[2 * j:2 * j + 2]
    for k in range(1, NY):
        yy = (y + k) % NY
        send(ys.at[yy], yr.at[k], yss.at[k], yrs.at[k], ydev(yy))

    for i in range(PAIRS):
        for way in range(2):
            ref = kvr.at[way, i]
            remote(ref, ref, ps.at[way, i], pr_.at[way, i], dev(left, d)).wait_recv()
        for j in range(2):
            g = kvp[i, j, mid, :].astype(F32) + kvr[0, i, j].astype(F32) + kvr[1, i, j].astype(F32)
            gkv[i, j] = g.astype(BF)
        store(gkv.at[i, 0], dk_h.at[0, :, pl.ds(i * PW, PW)], lo.at[5 + i])
        store(gkv.at[i, 1], dv_h.at[0, :, pl.ds(i * PW, PW)], lo.at[9 + i])

    final = ys[y]
    for k in range(1, NY):
        remote(yr.at[k], yr.at[k], yss.at[k], yrs.at[k], ydev((y + NY - k) % NY)).wait_recv()
        final = final + yr[k]
    gw[...] = final
    store(gw, gw_h, lo.at[13])
    for c in sends:
        c.wait_send()
    for c in outs:
        c.wait()


def on_device(queries, key_states, values, w_out, cotangent, neighbours, counts):
    big = jax.ShapeDtypeStruct((1, 128, 1024), BF)
    any_ = pl.BlockSpec(memory_space=pl.ANY)
    smem = pl.BlockSpec(memory_space=pltpu.SMEM)
    V, D = pltpu.VMEM, pltpu.SemaphoreType.DMA
    return pl.pallas_call(
        kernel,
        name="patch_attention",
        out_shape=(big, big, big, big, jax.ShapeDtypeStruct((2, 1024), F32)),
        in_specs=[smem, smem] + [any_] * 5,
        out_specs=[any_] * 5,
        scratch_shapes=[
            V((4, 128, 256), BF),
            V((4, 2, 384, 256), BF),
            V((4, 256, 1024), BF),
            V((8, 128, 1024), BF),
            V((4, 128, 256), BF),
            V((128, 1024), BF),
            V((4, 128, 256), BF),
            V((4, 2, 384, 256), BF),
            V((2, 4, 2, 128, 256), BF),
            V((4, 8, 32, 128), BF),
            V((8, 128, 128), BF),
            V((8, 16, 1024), BF),
            V((8, 16, 1024), BF),
            V((8, 2, 1024), F32),
            V((8, 2, 1024), F32),
            V((128, 1024), BF),
            V((4, 2, 128, 256), BF),
            V((2, 1024), F32),
            D((4,)), D((4, 2)), D((4,)), D, D((14,)),
            D((2, 4)), D((2, 4)), D((5, 2)), D((5, 2)), D((4, 8)), D((4, 8)),
            D((2, 4)), D((2, 4)), D((8,)), D((8,)), D((8,)), D((8,)),
        ],
        compiler_params=pltpu.CompilerParams(
            collective_id=0, has_side_effects=True, vmem_limit_bytes=60 * 1024 * 1024
        ),
    )(neighbours, counts, queries, key_states, values, w_out, cotangent)


def solution(mesh):
    placed = (
        P("dp", "seq", None),
        P("dp", "seq", None),
        P("dp", "seq", None),
        P(),
        P("dp", "seq", None),
        P("dp", "seq", None),
        P("dp", "seq"),
    )
    return jax.shard_map(
        on_device,
        mesh=mesh,
        in_specs=placed,
        out_specs=(
            P("dp", "seq", None),
            P("dp", "seq", None),
            P("dp", "seq", None),
            P("dp", "seq", None),
            P(("seq", "dp"), None),
        ),
        check_vma=False,
    )
```

time: 425 us -> 84.2 us (0.20)
  waiting for transfers between devices: 348 us -> 0 us
  Pallas kernels: 0 us -> 75.2 us
  local copies, waits for them, and re-layouts: 23.8 us -> 7.28 us
  between operations: 15.6 us -> 1.3 us
  starting transfers between devices: 14.1 us -> 0 us
  matrix products: 12.6 us -> 0 us
  other arithmetic: 6.76 us -> 0 us
    reduce_scatter x1 -> x0, waiting for transfers between devices: 225 us -> none  [on_device(): lax.psum_scatter(lax.optimization_barrier(term.astype(jnp.bfloat16)).asty...]
    unnamed x3 -> x0, waiting for transfers between devices: 113 us -> none
    pallas_call x0 -> x1, Pallas kernels: none -> 75.2 us  [on_device(): pl.pallas_call(kernel, name='patch_attention', out_shape=(big, big, big,...]
    ppermute x4 -> x0, starting transfers between devices: 14 us -> none  [passed_along(): return lax.ppermute(value, axis, pairs)]
    dot_general x9 -> x0, matrix products: 12.6 us -> none  [the longest x1 2.81 us: attend(): jnp.einsum('hqk,qhd->khd', probs_low, grad_heads, preferred_element_type=...]
    ppermute x4 -> x0, waiting for transfers between devices: 9.82 us -> none  [passed_along(): return lax.ppermute(value, axis, pairs)]
    convert_element_type x5 -> x0, local copies, waits for them, and re-layouts: 9.33 us -> none  [the longest x2 4.63 us: attend(): value_parts.reshape(-1, patch_rows, feature_count).astype(jnp.bfloat16)]
    unnamed x29 -> x7, local copies, waits for them, and re-layouts: 9.92 us -> 7.28 us
  transfers between devices with their start and end apart: 6 -> 0, of which waited for: 6 -> 0; matrix products, arithmetic and copies ran while one was open for 7% -> 0% of each run, Pallas kernels for 0% -> 0%
where the time goes in v1:
time: 84.2 us; the launch traced here: 83.8 us
  Pallas kernels  75.2 us (89%)
  local copies, waits for them, and re-layouts  7.28 us (9%)
  between operations  1.3 us (2%)
    pallas_call x1, Pallas kernels, on_device(): pl.pallas_call(kernel, name='patch_attention', out_shape=(big, big, big,...  75.2 us
    unnamed x7, local copies, waits for them, and re-layouts  7.28 us

profile of v1, /device:TPU:6, one launch (start us, length us, event | category | flops | bytes accessed | tf_op | source)
XLA Modules:
  0.0 83.8 jit_solution(3242650374999874046)
XLA Ops:
  1.3 75.2 %patch_attention.1 = (bf16[1,128,1024]{2,1,0:T(8,128)(2,1)}, bf16[1,128,1024]{2,1,0:T(8,128)(2,1)}, bf16[1,128,1024]{2,1,0:T(8,128)(2,1)}, bf16[1,128,1024]{2,1,0:T(8,128)(2,1)}, f32[2,1024]{1,0:T(2,128)}) custom-call(s32[1,1,2]{2,1,0:T(1,128)} %nbr.1, s32[1,1]{1,0:T(1,128)S(6)} %copy.17.cnt, bf16[1,128,1024]{2,1,0:T(8,128)(2,1)} %q_h.1, ...), custom_call_target="tpu_custom_call" | custom-call | tf_op jit(solution)/shard_map/patch_attention/pallas_call | solution.py:255
  76.5 0.0 copy-start
  76.5 1.7 %copy.18 = bf16[1,128,1024]{2,1,0:T(8,128)(2,1)} copy(bf16[1,128,1024]{2,1,0:T(8,128)(2,1)} %get-tuple-element.10) | data formatting | bytes 524288
  78.2 1.7 %copy.19 = bf16[1,128,1024]{2,1,0:T(8,128)(2,1)} copy(bf16[1,128,1024]{2,1,0:T(8,128)(2,1)} %get-tuple-element.11) | data formatting | bytes 524288
  79.9 1.7 %copy.20 = bf16[1,128,1024]{2,1,0:T(8,128)(2,1)} copy(bf16[1,128,1024]{2,1,0:T(8,128)(2,1)} %get-tuple-element.12) | data formatting | bytes 524288
  81.5 1.7 %copy.21 = bf16[1,128,1024]{2,1,0:T(8,128)(2,1)} copy(bf16[1,128,1024]{2,1,0:T(8,128)(2,1)} %get-tuple-element.13) | data formatting | bytes 524288
  83.2 0.0 copy-done
  83.2 0.6 copy.22
Async XLA Ops:
  76.5 6.7 %copy-start = (f32[2,1024]{1,0:T(2,128)S(1)}, f32[2,1024]{1,0:T(2,128)}, u32[]{:S(2)}) copy-start(f32[2,1024]{1,0:T(2,128)} %get-tuple-element.14) | copy-start | bytes 24580

commit v2 on v1

v2 whole, which is shorter than its diff:
```python
import math

import jax
import jax.numpy as jnp
from jax import lax
from jax.experimental import pallas as pl
from jax.experimental.pallas import tpu as pltpu
from jax.sharding import PartitionSpec as P

HD = 128
PAIRS = 4
PW = 2 * HD
BF = jnp.bfloat16
F32 = jnp.float32
NX, NY, NZ = 4, 8, 8
MESH = pl.DeviceIdType.MESH


def dot(a, b, ca, cb):
    return lax.dot_general(a, b, (((ca,), (cb,)), ((), ())), preferred_element_type=F32)


def kernel(
    nbr, cnt, q_h, k_h, v_h, w_h, c_h,
    out_r, dq_r, dk_r, dv_r, gw_r,
    q, kv, w, cot, do, att, kvp, kvr, asend, aall, zs, zr, ys, yr, rb, rb2,
    lq, lkv, lw, lc,
    hs, hr, cs, cr, as_, ar, ps, pr_, zss, zrs, yss, yrs, fs, fr, gs, gr,
):
    s = lax.axis_index("seq")
    d = lax.axis_index("dp")
    z_hi, y = s // NY, s % NY
    z_lo, xc = d // 8, d % 8
    x, core = xc // 2, xc % 2
    z = z_hi * 2 + z_lo

    def grp(j):
        return {"seq": s, "dp": z_lo * 8 + j}

    def zyd(zz, yy):
        return {"seq": (zz // 2) * NY + yy, "dp": (zz % 2) * 8 + xc}

    up, down = (z + 1) % NZ, (z + NZ - 1) % NZ
    yu, yd = (y + 1) % NY, (y + NY - 1) % NY

    barrier = pltpu.get_barrier_semaphore()
    peers = [zyd(up, yu), zyd(down, yd)]
    peers += [grp((xc + k) % 8) for k in range(1, 8)]
    peers += [zyd((z + k) % NZ, y) for k in range(1, NZ)]
    peers += [zyd(z, (y + k) % NY) for k in range(1, NY)]
    for peer in peers:
        pl.semaphore_signal(barrier, inc=1, device_id=peer, device_id_type=MESH)

    loads = {}

    def load(key, src, dst, sem):
        c = pltpu.make_async_copy(src, dst, sem)
        c.start()
        loads[key] = c

    load("c", c_h.at[0], cot.at[xc], lc)
    for i in range(PAIRS):
        load(("w", i), w_h.at[pl.ds(i * PW, PW), :], w.at[i], lw.at[i])
    for i in range(PAIRS):
        cols = pl.ds(i * PW, PW)
        load(("q", i), q_h.at[0, :, cols], q.at[i], lq.at[i])
        load(("k", i), k_h.at[0, :, cols], kv.at[i, 0, pl.ds(128, 128), :], lkv.at[i, 0])
        load(("v", i), v_h.at[0, :, cols], kv.at[i, 1, pl.ds(128, 128), :], lkv.at[i, 1])

    pl.semaphore_wait(barrier, len(peers))

    sends = []

    def remote(src, dst, ss, rs, to):
        return pltpu.make_async_remote_copy(
            src_ref=src, dst_ref=dst, send_sem=ss, recv_sem=rs, device_id=to, device_id_type=MESH
        )

    def send(*args):
        c = remote(*args)
        c.start()
        sends.append(c)

    mid = pl.ds(128, 128)
    side = (pl.ds(0, 128), pl.ds(256, 128))
    xr = ((x + 1) % NX) * 2 + core
    xl = ((x + 3) % NX) * 2 + core
    xo = ((x + 2) % NX) * 2 + core
    partner = x * 2 + (1 - core)
    half = (pl.ds(0, 64), pl.ds(64, 64))

    edge = (y == NY - 1, y == 0)
    next_y = (zyd(z, yu), zyd(z, yd))
    next_z = (zyd(up, y), zyd(down, y))
    next_zy = (zyd(up, yu), zyd(down, yd))

    def to_side(src, dst, relay, ss, rs, rrs, way):
        @pl.when(edge[way])
        def _():
            remote(src, relay, ss, rrs, next_z[way]).start()

        @pl.when(jnp.logical_not(edge[way]))
        def _():
            remote(src, dst, ss, rs, next_y[way]).start()

        sends.append(remote(src, dst, ss, rs, next_y[way]))

    def pass_on(relay, dsts, fss, rss, rrs):
        for way in range(2):
            @pl.when(edge[way])
            def _():
                remote(relay, relay, fss, rrs, next_z[way]).wait_recv()
                remote(relay, dsts[way], fss, rss[way], next_zy[way]).start()

    srcs = (k_h, v_h)

    def halo(i, j, way):
        to_side(
            srcs[j].at[0, :, pl.ds(i * PW, PW)], kv.at[i, j, side[way], :], rb.at[i, j],
            hs.at[way, j, i], hr.at[way, j, i], fr.at[i, j], way,
        )

    for i in range(PAIRS):
        for j in range(2):
            for way in range(2):
                halo(i, j, way)
        if i == 0:
            for n, (to, first) in enumerate(((xr, 0), (xl, 1))):
                for m, hh in enumerate((first, 1 - first)):
                    send(c_h.at[0, half[hh], :], cot.at[xc, half[hh], :], cs.at[n, m], cr.at[n, m], grp(to))
            send(c_h.at[0], cot.at[xc], cs.at[2, 0], cr.at[2, 0], grp(partner))

    loads["c"].wait()
    c_own = cot[xc]
    for i in range(PAIRS):
        loads["w", i].wait()
        do[i] = dot(c_own, w[i], 1, 1).astype(BF)
    for i in range(PAIRS):
        for key in "qkv":
            loads[key, i].wait()

    n0, n1, live = nbr[0, 0, 0], nbr[0, 0, 1], cnt[0, 0]

    def bias(target):
        hit = ((n0 == target) & (live > 0)) | ((n1 == target) & (live > 1))
        return jnp.where(hit, 0.0, -jnp.inf).astype(F32)

    b_left, b_right = bias(s - 1), bias(s + 1)
    scale = 1.0 / math.sqrt(HD)

    o_id = lax.broadcasted_iota(jnp.int32, (PW, PW), 0)
    f_id = lax.broadcasted_iota(jnp.int32, (PW, PW), 1)
    f_of = ((o_id >> 1) & 7) * 32 + ((o_id >> 4) & 1) * 16 + ((o_id >> 5) & 7) * 2 + (o_id & 1)
    perm = jnp.where(f_id == f_of, 1.0, 0.0).astype(BF)

    def cot_wait(slot, rows, n, m):
        ref = cot.at[slot] if rows is None else cot.at[slot, half[rows], :]
        remote(ref, ref, cs.at[n, m], cr.at[n, m], grp(partner)).wait_recv()

    for i in range(PAIRS):
        for j in range(2):
            pass_on(
                rb.at[i, j], [kv.at[i, j, side[way], :] for way in range(2)],
                fs.at[i, j], [hr.at[way, j, i] for way in range(2)], fr.at[i, j],
            )
        for j in range(2):
            for way in range(2):
                ref = kv.at[i, j, side[way], :]
                remote(ref, ref, hs.at[way, j, i], hr.at[way, j, i], next_y[way]).wait_recv()
        kept = []
        for h in range(2):
            cols = pl.ds(h * HD, HD)
            qh, kh, vh = q[i, :, cols], kv[i, 0, :, cols], kv[i, 1, :, cols]
            t = dot(kh, qh, 1, 1) * scale
            t = jnp.concatenate([t[:128] + b_left, t[128:256], t[256:] + b_right], axis=0)
            e = jnp.exp(t - jnp.max(t, axis=0, keepdims=True))
            p = e * (1.0 / jnp.sum(e, axis=0, keepdims=True))
            pb = p.astype(BF)
            att[:, pl.ds(i * PW + h * HD, HD)] = dot(pb, vh, 0, 0).astype(BF)
            kept.append((p, pb))
        a_pair = att[:, pl.ds(i * PW, PW)]
        asend[i] = dot(perm, a_pair, 1, 1).astype(BF).reshape(8, 32, 128)
        rows = pl.ds(i * 32, 32)
        for k in range(1, 8):
            j = (xc + k) % 8
            send(asend.at[i, j], aall.at[xc, rows, :], as_.at[i, k], ar.at[i, k], grp(j))
        aall[xc, rows, :] = asend[i, xc]
        for h in range(2):
            cols = pl.ds(h * HD, HD)
            qh, doh = q[i, :, cols], do[i, :, cols]
            kh, vh = kv[i, 0, :, cols], kv[i, 1, :, cols]
            p, pb = kept[h]
            dp = dot(vh, doh, 1, 1)
            delta = jnp.sum(p * dp, axis=0, keepdims=True)
            ds = (p * (dp - delta)).astype(BF)
            kvp[i, 0, :, cols] = (dot(ds, qh, 1, 0) * scale).astype(BF)
            kvp[i, 1, :, cols] = dot(pb, doh, 1, 0).astype(BF)
            dq_r[0, :, pl.ds(i * PW + h * HD, HD)] = (dot(ds, kh, 0, 0) * scale).astype(BF)
        for j in range(2):
            for way in range(2):
                to_side(
                    kvp.at[i, j, side[1 - way], :], kvr.at[way, i, j], rb2.at[i, j],
                    ps.at[way, j, i], pr_.at[way, j, i], gr.at[i, j], way,
                )
        if i == 0:
            cot_wait(xl, 0, 0, 0)
            ref = cot.at[xl, half[0], :]
            send(ref, ref, cs.at[3, 0], cr.at[3, 0], grp(xr))
            cot_wait(xr, 1, 1, 0)
            ref = cot.at[xr, half[1], :]
            send(ref, ref, cs.at[3, 1], cr.at[3, 1], grp(xl))
        if i == 2:
            cot_wait(xl, 1, 0, 1)
            send(cot.at[xl], cot.at[xl], cs.at[4, 0], cr.at[4, 0], grp(partner))
            cot_wait(xr, 0, 1, 1)
            send(cot.at[xr], cot.at[xr], cs.at[4, 1], cr.at[4, 1], grp(partner))
            cot_wait(xo, 0, 3, 0)
            cot_wait(xo, 1, 3, 1)
            send(cot.at[xo], cot.at[xo], cs.at[2, 1], cr.at[2, 1], grp(partner))

    def flip(slot):
        return (slot // 2) * 2 + (1 - slot % 2)

    cot_wait(partner, None, 2, 0)
    cot_wait(flip(xl), None, 4, 0)
    cot_wait(flip(xr), None, 4, 1)
    cot_wait(flip(xo), None, 2, 1)
    c_all = cot[...].reshape(1024, 1024)

    def zcopy(zz):
        return remote(zs.at[zz], zr.at[z], zss.at[zz], zrs.at[z], zyd(jnp.int32(zz), y))

    def reduce_rows(first, last):
        for i in range(first, last):
            for k in range(1, 8):
                j = (xc + 8 - k) % 8
                ref = aall.at[j, pl.ds(i * 32, 32), :]
                remote(ref, ref, as_.at[i, k], ar.at[i, k], grp(j)).wait_recv()
        a_t = jnp.concatenate([aall[j, pl.ds(first * 32, (last - first) * 32), :] for j in range(8)], axis=1)
        term = dot(a_t, c_all, 1, 0).astype(BF).reshape((last - first) * 2, 16, 1024)
        zs[pl.ds(first * 2, (last - first) * 2)] = term
        for zz in range(first * 2, last * 2):
            @pl.when(z != zz)
            def _():
                zcopy(zz).start()

    def pass_parts(i):
        for j in range(2):
            pass_on(
                rb2.at[i, j], [kvr.at[way, i, j] for way in range(2)],
                gs.at[i, j], [pr_.at[way, j, i] for way in range(2)], gr.at[i, j],
            )

    reduce_rows(0, 3)
    a_all = att[...]
    out_r[0] = sum(dot(a_all[:, i * PW:(i + 1) * PW], w[i], 1, 0) for i in range(PAIRS)).astype(BF)
    pass_parts(0)
    reduce_rows(3, 4)
    for i in range(1, PAIRS):
        pass_parts(i)
    zr[z] = zs[z]
    for zz in range(NZ):
        @pl.when(z != zz)
        def _():
            remote(zr.at[zz], zr.at[zz], zss.at[zz], zrs.at[zz], zyd(jnp.int32(zz), y)).wait_recv()
    total = sum(zr[zz].astype(F32) for zz in range(NZ))
    for j in range(NY):
        ys[j] = total[2 * j:2 * j + 2]
    for k in range(1, NY):
        yy = (y + k) % NY
        send(ys.at[yy], yr.at[k], yss.at[k], yrs.at[k], zyd(z, yy))

    for i in range(PAIRS):
        for j, ref in enumerate((dk_r, dv_r)):
            for way in range(2):
                got = kvr.at[way, i, j]
                remote(got, got, ps.at[way, j, i], pr_.at[way, j, i], next_y[way]).wait_recv()
            g = kvp[i, j, mid, :].astype(F32) + kvr[0, i, j].astype(F32) + kvr[1, i, j].astype(F32)
            ref[0, :, pl.ds(i * PW, PW)] = g.astype(BF)

    final = ys[y]
    for k in range(1, NY):
        remote(yr.at[k], yr.at[k], yss.at[k], yrs.at[k], zyd(z, (y + NY - k) % NY)).wait_recv()
        final = final + yr[k]
    gw_r[...] = final
    for c in sends:
        c.wait_send()
    for zz in range(NZ):
        @pl.when(z != zz)
        def _():
            zcopy(zz).wait_send()

    @pl.when(edge[0] | edge[1])
    def _():
        for i in range(PAIRS):
            for j in range(2):
                remote(rb.at[i, j], rb.at[i, j], fs.at[i, j], fr.at[i, j], next_y[0]).wait_send()
                remote(rb2.at[i, j], rb2.at[i, j], gs.at[i, j], gr.at[i, j], next_y[0]).wait_send()


def flush(*refs):
    sem = refs[-1]
    copies = [pltpu.make_async_copy(refs[n], refs[5 + n], sem.at[n]) for n in range(5)]
    for c in copies:
        c.start()
    for c in copies:
        c.wait()


def on_device(queries, key_states, values, w_out, cotangent, neighbours, counts):
    big = jax.ShapeDtypeStruct((1, 128, 1024), BF)
    hbm = pl.BlockSpec(memory_space=pltpu.HBM)
    vmem = pl.BlockSpec(memory_space=pltpu.VMEM)
    smem = pl.BlockSpec(memory_space=pltpu.SMEM)
    V, D = pltpu.VMEM, pltpu.SemaphoreType.DMA
    results = pl.pallas_call(
        kernel,
        name="patch_attention",
        out_shape=(V((1, 128, 1024), BF),) * 4 + (V((2, 1024), F32),),
        in_specs=[smem, smem] + [hbm] * 5,
        out_specs=[vmem] * 5,
        scratch_shapes=[
            V((4, 128, 256), BF),
            V((4, 2, 384, 256), BF),
            V((4, 256, 1024), BF),
            V((8, 128, 1024), BF),
            V((4, 128, 256), BF),
            V((128, 1024), BF),
            V((4, 2, 384, 256), BF),
            V((2, 4, 2, 128, 256), BF),
            V((4, 8, 32, 128), BF),
            V((8, 128, 128), BF),
            V((8, 16, 1024), BF),
            V((8, 16, 1024), BF),
            V((8, 2, 1024), F32),
            V((8, 2, 1024), F32),
            V((4, 2, 128, 256), BF),
            V((4, 2, 128, 256), BF),
            D((4,)), D((4, 2)), D((4,)), D,
            D((2, 2, 4)), D((2, 2, 4)), D((5, 2)), D((5, 2)), D((4, 8)), D((4, 8)),
            D((2, 2, 4)), D((2, 2, 4)), D((8,)), D((8,)), D((8,)), D((8,)),
            D((4, 2)), D((4, 2)), D((4, 2)), D((4, 2)),
        ],
        compiler_params=pltpu.CompilerParams(
            collective_id=0, has_side_effects=True, vmem_limit_bytes=65_000_000
        ),
    )(neighbours, counts, queries, key_states, values, w_out, cotangent)
    return pl.pallas_call(
        flush,
        name="flush",
        out_shape=(big, big, big, big, jax.ShapeDtypeStruct((2, 1024), F32)),
        in_specs=[vmem] * 5,
        out_specs=[hbm] * 5,
        scratch_shapes=[D((5,))],
        compiler_params=pltpu.CompilerParams(vmem_limit_bytes=4_000_000),
    )(*results)


def solution(mesh):
    placed = (
        P("dp", "seq", None),
        P("dp", "seq", None),
        P("dp", "seq", None),
        P(),
        P("dp", "seq", None),
        P("dp", "seq", None),
        P("dp", "seq"),
    )
    return jax.shard_map(
        on_device,
        mesh=mesh,
        in_specs=placed,
        out_specs=(
            P("dp", "seq", None),
            P("dp", "seq", None),
            P("dp", "seq", None),
            P("dp", "seq", None),
            P(("seq", "dp"), None),
        ),
        check_vma=False,
    )
```

time: 84.2 us -> 71.6 us (0.85)
  local copies, waits for them, and re-layouts: 7.28 us -> 0 us
  Pallas kernels: 75.2 us -> 70.2 us
    unnamed x7 -> x0, local copies, waits for them, and re-layouts: 7.28 us -> none
    pallas_call x1 -> x2, Pallas kernels: 75.2 us -> 70.2 us  [the longest x1 69.2 us: on_device(): pl.pallas_call(kernel, name='patch_attention', out_shape=(V((1, 128, 1024...]
where the time goes in v2:
time: 71.6 us; the launch traced here: 71.5 us
  Pallas kernels  70.2 us (98%)
  between operations  1.29 us (2%)
    pallas_call x1, Pallas kernels, on_device(): pl.pallas_call(kernel, name='patch_attention', out_shape=(V((1, 128, 1024...  69.2 us

profile of v2, /device:TPU:6, one launch (start us, length us, event | category | flops | bytes accessed | tf_op | source)
XLA Modules:
  0.0 71.5 jit_solution(15287028846950007513)
XLA Ops:
  1.3 69.2 %patch_attention.1 = (bf16[1,128,1024]{2,1,0:T(8,128)(2,1)S(1)}, bf16[1,128,1024]{2,1,0:T(8,128)(2,1)S(1)}, bf16[1,128,1024]{2,1,0:T(8,128)(2,1)S(1)}, bf16[1,128,1024]{2,1,0:T(8,128)(2,1)S(1)}, f32[2,1024]{1,0:T(2,128)S(1)}) custom-call(s32[1,1,2]{2,1,0:T(1,128)} %nbr.1, s32[1,1]{1,0:T(1,128)S(6)} %copy.12.cnt, bf16[1,128,1024]{2,1,0:T(8,128)(2,1)} %q_h.1, ...), custom_call_target="tpu_custom_call" | custom-call | tf_op jit(solution)/shard_map/patch_attention/pallas_call | solution.py:316
  70.4 1.0 %flush.1 = (bf16[1,128,1024]{2,1,0:T(8,128)(2,1)}, bf16[1,128,1024]{2,1,0:T(8,128)(2,1)}, bf16[1,128,1024]{2,1,0:T(8,128)(2,1)}, bf16[1,128,1024]{2,1,0:T(8,128)(2,1)}, f32[2,1024]{1,0:T(2,128)}) custom-call(bf16[1,128,1024]{2,1,0:T(8,128)(2,1)S(1)} %get-tuple-element.10.refs_0_, bf16[1,128,1024]{2,1,0:T(8,128)(2,1)S(1)} %get-tuple-element.11.refs_1_, ...), custom_call_target="tpu_custom_call" | custom-call | tf_op jit(solution)/shard_map/flush/pallas_call | solution.py:348

commit v3 on v2

--- a/solution.py
+++ b/solution.py
@@ -23,9 +23,9 @@
 def kernel(
     nbr, cnt, q_h, k_h, v_h, w_h, c_h,
     out_r, dq_r, dk_r, dv_r, gw_r,
-    q, kv, w, cot, do, att, kvp, kvr, asend, aall, zs, zr, ys, yr, rb, rb2,
+    q, kv, w, cot, do, att, kvp, kvr, asend, aall, zs, zr, rb, rb2,
     lq, lkv, lw, lc,
-    hs, hr, cs, cr, as_, ar, ps, pr_, zss, zrs, yss, yrs, fs, fr, gs, gr,
+    hs, hr, cs, cr, as_, ar, ps, pr_, zss, zrs, fs, fr, gs, gr,
 ):
     s = lax.axis_index("seq")
     d = lax.axis_index("dp")
@@ -44,12 +44,18 @@
     yu, yd = (y + 1) % NY, (y + NY - 1) % NY
 
     barrier = pltpu.get_barrier_semaphore()
-    peers = [zyd(up, yu), zyd(down, yd)]
-    peers += [grp((xc + k) % 8) for k in range(1, 8)]
-    peers += [zyd((z + k) % NZ, y) for k in range(1, NZ)]
-    peers += [zyd(z, (y + k) % NY) for k in range(1, NY)]
-    for peer in peers:
-        pl.semaphore_signal(barrier, inc=1, device_id=peer, device_id_type=MESH)
+    me = z * NY + y
+
+    def place(c):
+        return zyd(c // NY, c % NY)
+
+    def greet(k, carry):
+        pl.semaphore_signal(barrier, inc=1, device_id=place((me + k) % 64), device_id_type=MESH)
+        return carry
+
+    for k in range(1, 8):
+        pl.semaphore_signal(barrier, inc=1, device_id=grp((xc + k) % 8), device_id_type=MESH)
+    lax.fori_loop(1, 64, greet, 0)
 
     loads = {}
 
@@ -67,7 +73,7 @@
         load(("k", i), k_h.at[0, :, cols], kv.at[i, 0, pl.ds(128, 128), :], lkv.at[i, 0])
         load(("v", i), v_h.at[0, :, cols], kv.at[i, 1, pl.ds(128, 128), :], lkv.at[i, 1])
 
-    pl.semaphore_wait(barrier, len(peers))
+    pl.semaphore_wait(barrier, 70)
 
     sends = []
 
@@ -128,7 +134,8 @@
             for n, (to, first) in enumerate(((xr, 0), (xl, 1))):
                 for m, hh in enumerate((first, 1 - first)):
                     send(c_h.at[0, half[hh], :], cot.at[xc, half[hh], :], cs.at[n, m], cr.at[n, m], grp(to))
-            send(c_h.at[0], cot.at[xc], cs.at[2, 0], cr.at[2, 0], grp(partner))
+
+    send(c_h.at[0], cot.at[xc], cs.at[2, 0], cr.at[2, 0], grp(partner))
 
     loads["c"].wait()
     c_own = cot[xc]
@@ -157,12 +164,61 @@
         ref = cot.at[slot] if rows is None else cot.at[slot, half[rows], :]
         remote(ref, ref, cs.at[n, m], cr.at[n, m], grp(partner)).wait_recv()
 
-    for i in range(PAIRS):
+    def pass_halo(i):
         for j in range(2):
             pass_on(
                 rb.at[i, j], [kv.at[i, j, side[way], :] for way in range(2)],
                 fs.at[i, j], [hr.at[way, j, i] for way in range(2)], fr.at[i, j],
             )
+
+    def flip(slot):
+        return (slot // 2) * 2 + (1 - slot % 2)
+
+    def chunk(c):
+        return remote(zs.at[c], zr.at[(me + 64 - c) % 64], zss, zrs, place(c))
+
+    def reduce_rows(first, last):
+        for i in range(first, last):
+            for k in range(1, 8):
+                j = (xc + 8 - k) % 8
+                ref = aall.at[j, pl.ds(i * 32, 32), :]
+                remote(ref, ref, as_.at[i, k], ar.at[i, k], grp(j)).wait_recv()
+        a_t = jnp.concatenate([aall[j, pl.ds(first * 32, (last - first) * 32), :] for j in range(8)], axis=1)
+        term = dot(a_t, cot[...].reshape(1024, 1024), 1, 0)
+        count = (last - first) * 16
+        zs[pl.ds(first * 16, count)] = term.reshape(count, 16, 128).astype(BF)
+
+        def hand_out(k, carry):
+            c = first * 16 + (me + k) % count
+
+            @pl.when(c != me)
+            def _():
+                chunk(c).start()
+
+            return carry
+
+        lax.fori_loop(0, count, hand_out, 0)
+
+    def pass_parts(i):
+        for j in range(2):
+            pass_on(
+                rb2.at[i, j], [kvr.at[way, i, j] for way in range(2)],
+                gs.at[i, j], [pr_.at[way, j, i] for way in range(2)], gr.at[i, j],
+            )
+
+    def return_parts(i):
+        for j in range(2):
+            for way in range(2):
+                to_side(
+                    kvp.at[i, j, side[1 - way], :], kvr.at[way, i, j], rb2.at[i, j],
+                    ps.at[way, j, i], pr_.at[way, j, i], gr.at[i, j], way,
+                )
+
+    pass_halo(0)
+    pass_halo(1)
+    for i in range(PAIRS):
+        if i + 2 < PAIRS:
+            pass_halo(i + 2)
         for j in range(2):
             for way in range(2):
                 ref = kv.at[i, j, side[way], :]
@@ -185,6 +241,10 @@
             j = (xc + k) % 8
             send(asend.at[i, j], aall.at[xc, rows, :], as_.at[i, k], ar.at[i, k], grp(j))
         aall[xc, rows, :] = asend[i, xc]
+        if i == 2:
+            cot_wait(xo, 0, 3, 0)
+            cot_wait(xo, 1, 3, 1)
+            send(cot.at[xo], cot.at[xo], cs.at[2, 1], cr.at[2, 1], grp(partner))
         for h in range(2):
             cols = pl.ds(h * HD, HD)
             qh, doh = q[i, :, cols], do[i, :, cols]
@@ -196,12 +256,7 @@
             kvp[i, 0, :, cols] = (dot(ds, qh, 1, 0) * scale).astype(BF)
             kvp[i, 1, :, cols] = dot(pb, doh, 1, 0).astype(BF)
             dq_r[0, :, pl.ds(i * PW + h * HD, HD)] = (dot(ds, kh, 0, 0) * scale).astype(BF)
-        for j in range(2):
-            for way in range(2):
-                to_side(
-                    kvp.at[i, j, side[1 - way], :], kvr.at[way, i, j], rb2.at[i, j],
-                    ps.at[way, j, i], pr_.at[way, j, i], gr.at[i, j], way,
-                )
+        return_parts(i)
         if i == 0:
             cot_wait(xl, 0, 0, 0)
             ref = cot.at[xl, half[0], :]
@@ -209,67 +264,24 @@
             cot_wait(xr, 1, 1, 0)
             ref = cot.at[xr, half[1], :]
             send(ref, ref, cs.at[3, 1], cr.at[3, 1], grp(xl))
-        if i == 2:
+        if i == 1:
             cot_wait(xl, 1, 0, 1)
             send(cot.at[xl], cot.at[xl], cs.at[4, 0], cr.at[4, 0], grp(partner))
             cot_wait(xr, 0, 1, 1)
             send(cot.at[xr], cot.at[xr], cs.at[4, 1], cr.at[4, 1], grp(partner))
-            cot_wait(xo, 0, 3, 0)
-            cot_wait(xo, 1, 3, 1)
-            send(cot.at[xo], cot.at[xo], cs.at[2, 1], cr.at[2, 1], grp(partner))
-
-    def flip(slot):
-        return (slot // 2) * 2 + (1 - slot % 2)
-
+
+    pass_parts(0)
     cot_wait(partner, None, 2, 0)
     cot_wait(flip(xl), None, 4, 0)
     cot_wait(flip(xr), None, 4, 1)
     cot_wait(flip(xo), None, 2, 1)
-    c_all = cot[...].reshape(1024, 1024)
-
-    def zcopy(zz):
-        return remote(zs.at[zz], zr.at[z], zss.at[zz], zrs.at[z], zyd(jnp.int32(zz), y))
-
-    def reduce_rows(first, last):
-        for i in range(first, last):
-            for k in range(1, 8):
-                j = (xc + 8 - k) % 8
-                ref = aall.at[j, pl.ds(i * 32, 32), :]
-                remote(ref, ref, as_.at[i, k], ar.at[i, k], grp(j)).wait_recv()
-        a_t = jnp.concatenate([aall[j, pl.ds(first * 32, (last - first) * 32), :] for j in range(8)], axis=1)
-        term = dot(a_t, c_all, 1, 0).astype(BF).reshape((last - first) * 2, 16, 1024)
-        zs[pl.ds(first * 2, (last - first) * 2)] = term
-        for zz in range(first * 2, last * 2):
-            @pl.when(z != zz)
-            def _():
-                zcopy(zz).start()
-
-    def pass_parts(i):
-        for j in range(2):
-            pass_on(
-                rb2.at[i, j], [kvr.at[way, i, j] for way in range(2)],
-                gs.at[i, j], [pr_.at[way, j, i] for way in range(2)], gr.at[i, j],
-            )
-
     reduce_rows(0, 3)
     a_all = att[...]
     out_r[0] = sum(dot(a_all[:, i * PW:(i + 1) * PW], w[i], 1, 0) for i in range(PAIRS)).astype(BF)
-    pass_parts(0)
     reduce_rows(3, 4)
-    for i in range(1, PAIRS):
-        pass_parts(i)
-    zr[z] = zs[z]
-    for zz in range(NZ):
-        @pl.when(z != zz)
-        def _():
-            remote(zr.at[zz], zr.at[zz], zss.at[zz], zrs.at[zz], zyd(jnp.int32(zz), y)).wait_recv()
-    total = sum(zr[zz].astype(F32) for zz in range(NZ))
-    for j in range(NY):
-        ys[j] = total[2 * j:2 * j + 2]
-    for k in range(1, NY):
-        yy = (y + k) % NY
-        send(ys.at[yy], yr.at[k], yss.at[k], yrs.at[k], zyd(z, yy))
-
+    pass_parts(1)
+    pass_parts(2)
+    pass_parts(3)
     for i in range(PAIRS):
         for j, ref in enumerate((dk_r, dv_r)):
             for way in range(2):
@@ -278,17 +290,14 @@
             g = kvp[i, j, mid, :].astype(F32) + kvr[0, i, j].astype(F32) + kvr[1, i, j].astype(F32)
             ref[0, :, pl.ds(i * PW, PW)] = g.astype(BF)
 
-    final = ys[y]
-    for k in range(1, NY):
-        remote(yr.at[k], yr.at[k], yss.at[k], yrs.at[k], zyd(z, (y + NY - k) % NY)).wait_recv()
-        final = final + yr[k]
-    gw_r[...] = final
+    everyone = pl.ds(1, 63)
+    remote(zs.at[everyone], zr.at[everyone], zss, zrs, next_y[0]).wait_recv()
+    final = zs[me].astype(F32) + jnp.sum(zr[everyone].astype(F32), axis=0)
+    for j in range(8):
+        gw_r[:, pl.ds(j * 128, 128)] = jnp.concatenate([final[j:j + 1], final[8 + j:9 + j]], axis=0)
     for c in sends:
         c.wait_send()
-    for zz in range(NZ):
-        @pl.when(z != zz)
-        def _():
-            zcopy(zz).wait_send()
+    remote(zs.at[everyone], zr.at[everyone], zss, zrs, next_y[0]).wait_send()
 
     @pl.when(edge[0] | edge[1])
     def _():
@@ -330,15 +339,13 @@
             V((2, 4, 2, 128, 256), BF),
             V((4, 8, 32, 128), BF),
             V((8, 128, 128), BF),
-            V((8, 16, 1024), BF),
-            V((8, 16, 1024), BF),
-            V((8, 2, 1024), F32),
-            V((8, 2, 1024), F32),
+            V((64, 16, 128), BF),
+            V((64, 16, 128), BF),
             V((4, 2, 128, 256), BF),
             V((4, 2, 128, 256), BF),
             D((4,)), D((4, 2)), D((4,)), D,
             D((2, 2, 4)), D((2, 2, 4)), D((5, 2)), D((5, 2)), D((4, 8)), D((4, 8)),
-            D((2, 2, 4)), D((2, 2, 4)), D((8,)), D((8,)), D((8,)), D((8,)),
+            D((2, 2, 4)), D((2, 2, 4)), D, D,
             D((4, 2)), D((4, 2)), D((4, 2)), D((4, 2)),
         ],
         compiler_params=pltpu.CompilerParams(

time: 71.6 us -> 61.7 us (0.86); the launches traced: 71.5 us -> 60.7 us
  Pallas kernels: 70.2 us -> 59.4 us
    pallas_call x1, Pallas kernels: 69.2 us -> 58.4 us  [on_device(): pl.pallas_call(kernel, name='patch_attention', out_shape=(V((1, 128, 1024...]
where the time goes in v3:
time: 61.7 us; the launch traced here: 60.7 us
  Pallas kernels  59.4 us (96%)
  between operations  1.29 us (2%)
    pallas_call x1, Pallas kernels, on_device(): pl.pallas_call(kernel, name='patch_attention', out_shape=(V((1, 128, 1024...  58.4 us

profile of v3, /device:TPU:6, one launch (start us, length us, event | category | flops | bytes accessed | tf_op | source)
XLA Modules:
  0.0 60.7 jit_solution(4649296848341087118)
XLA Ops:
  1.3 58.4 %patch_attention.1 = (bf16[1,128,1024]{2,1,0:T(8,128)(2,1)S(1)}, bf16[1,128,1024]{2,1,0:T(8,128)(2,1)S(1)}, bf16[1,128,1024]{2,1,0:T(8,128)(2,1)S(1)}, bf16[1,128,1024]{2,1,0:T(8,128)(2,1)S(1)}, f32[2,1024]{1,0:T(2,128)S(1)}) custom-call(s32[1,1,2]{2,1,0:T(1,128)} %nbr.1, s32[1,1]{1,0:T(1,128)S(6)} %copy.12.cnt, bf16[1,128,1024]{2,1,0:T(8,128)(2,1)} %q_h.1, ...), custom_call_target="tpu_custom_call" | custom-call | tf_op jit(solution)/shard_map/patch_attention/pallas_call | solution.py:325
  59.7 1.0 %flush.1 = (bf16[1,128,1024]{2,1,0:T(8,128)(2,1)}, bf16[1,128,1024]{2,1,0:T(8,128)(2,1)}, bf16[1,128,1024]{2,1,0:T(8,128)(2,1)}, bf16[1,128,1024]{2,1,0:T(8,128)(2,1)}, f32[2,1024]{1,0:T(2,128)}) custom-call(bf16[1,128,1024]{2,1,0:T(8,128)(2,1)S(1)} %get-tuple-element.10.refs_0_, bf16[1,128,1024]{2,1,0:T(8,128)(2,1)S(1)} %get-tuple-element.11.refs_1_, ...), custom_call_target="tpu_custom_call" | custom-call | tf_op jit(solution)/shard_map/flush/pallas_call | solution.py:355

commit v4 on v3

--- a/solution.py
+++ b/solution.py
@@ -21,11 +21,11 @@
 
 
 def kernel(
-    nbr, cnt, q_h, k_h, v_h, w_h, c_h,
+    nbr_h, cnt, q_h, k_h, v_h, w_h, c_h,
     out_r, dq_r, dk_r, dv_r, gw_r,
     q, kv, w, cot, do, att, kvp, kvr, asend, aall, zs, zr, rb, rb2,
     lq, lkv, lw, lc,
-    hs, hr, cs, cr, as_, ar, ps, pr_, zss, zrs, fs, fr, gs, gr,
+    hs, hr, cs, cr, as_, ar, ps, pr_, zss, zrs, fs, fr, gs, gr, far, nbr, ln,
 ):
     s = lax.axis_index("seq")
     d = lax.axis_index("dp")
@@ -49,13 +49,12 @@
     def place(c):
         return zyd(c // NY, c % NY)
 
-    def greet(k, carry):
-        pl.semaphore_signal(barrier, inc=1, device_id=place((me + k) % 64), device_id_type=MESH)
-        return carry
-
-    for k in range(1, 8):
-        pl.semaphore_signal(barrier, inc=1, device_id=grp((xc + k) % 8), device_id_type=MESH)
-    lax.fori_loop(1, 64, greet, 0)
+    peers = [zyd(up, yu), zyd(down, yd)]
+    peers += [grp((xc + k) % 8) for k in range(1, 8)]
+    peers += [zyd((z + k) % NZ, y) for k in range(1, NZ)]
+    peers += [zyd(z, (y + k) % NY) for k in range(1, NY)]
+    for peer in peers:
+        pl.semaphore_signal(barrier, inc=1, device_id=peer, device_id_type=MESH)
 
     loads = {}
 
@@ -64,6 +63,7 @@
         c.start()
         loads[key] = c
 
+    load("n", nbr_h, nbr, ln)
     load("c", c_h.at[0], cot.at[xc], lc)
     for i in range(PAIRS):
         load(("w", i), w_h.at[pl.ds(i * PW, PW), :], w.at[i], lw.at[i])
@@ -73,7 +73,7 @@
         load(("k", i), k_h.at[0, :, cols], kv.at[i, 0, pl.ds(128, 128), :], lkv.at[i, 0])
         load(("v", i), v_h.at[0, :, cols], kv.at[i, 1, pl.ds(128, 128), :], lkv.at[i, 1])
 
-    pl.semaphore_wait(barrier, 70)
+    pl.semaphore_wait(barrier, len(peers))
 
     sends = []
 
@@ -137,6 +137,9 @@
 
     send(c_h.at[0], cot.at[xc], cs.at[2, 0], cr.at[2, 0], grp(partner))
 
+    for k in range(1, NY):
+        pl.semaphore_signal(far, inc=1, device_id=zyd(z, (y + k) % NY), device_id_type=MESH)
+
     loads["c"].wait()
     c_own = cot[xc]
     for i in range(PAIRS):
@@ -146,6 +149,7 @@
         for key in "qkv":
             loads[key, i].wait()
 
+    loads["n"].wait()
     n0, n1, live = nbr[0, 0, 0], nbr[0, 0, 1], cnt[0, 0]
 
     def bias(target):
@@ -245,6 +249,8 @@
             cot_wait(xo, 0, 3, 0)
             cot_wait(xo, 1, 3, 1)
             send(cot.at[xo], cot.at[xo], cs.at[2, 1], cr.at[2, 1], grp(partner))
+        if i == 3:
+            pass_parts(0)
         for h in range(2):
             cols = pl.ds(h * HD, HD)
             qh, doh = q[i, :, cols], do[i, :, cols]
@@ -270,18 +276,18 @@
             cot_wait(xr, 0, 1, 1)
             send(cot.at[xr], cot.at[xr], cs.at[4, 1], cr.at[4, 1], grp(partner))
 
-    pass_parts(0)
+    pass_parts(1)
+    a_all = att[...]
+    out_r[0] = sum(dot(a_all[:, i * PW:(i + 1) * PW], w[i], 1, 0) for i in range(PAIRS)).astype(BF)
+    pass_parts(2)
     cot_wait(partner, None, 2, 0)
     cot_wait(flip(xl), None, 4, 0)
     cot_wait(flip(xr), None, 4, 1)
     cot_wait(flip(xo), None, 2, 1)
-    reduce_rows(0, 3)
-    a_all = att[...]
-    out_r[0] = sum(dot(a_all[:, i * PW:(i + 1) * PW], w[i], 1, 0) for i in range(PAIRS)).astype(BF)
-    reduce_rows(3, 4)
-    pass_parts(1)
-    pass_parts(2)
+    pl.semaphore_wait(far, NY - 1)
+    reduce_rows(0, 4)
     pass_parts(3)
+
     for i in range(PAIRS):
         for j, ref in enumerate((dk_r, dv_r)):
             for way in range(2):
@@ -326,7 +332,7 @@
         kernel,
         name="patch_attention",
         out_shape=(V((1, 128, 1024), BF),) * 4 + (V((2, 1024), F32),),
-        in_specs=[smem, smem] + [hbm] * 5,
+        in_specs=[hbm, smem] + [hbm] * 5,
         out_specs=[vmem] * 5,
         scratch_shapes=[
             V((4, 128, 256), BF),
@@ -346,7 +352,8 @@
             D((4,)), D((4, 2)), D((4,)), D,
             D((2, 2, 4)), D((2, 2, 4)), D((5, 2)), D((5, 2)), D((4, 8)), D((4, 8)),
             D((2, 2, 4)), D((2, 2, 4)), D, D,
-            D((4, 2)), D((4, 2)), D((4, 2)), D((4, 2)),
+            D((4, 2)), D((4, 2)), D((4, 2)), D((4, 2)), pltpu.SemaphoreType.REGULAR,
+            pltpu.SMEM((1, 1, 2), jnp.int32), D,
         ],
         compiler_params=pltpu.CompilerParams(
             collective_id=0, has_side_effects=True, vmem_limit_bytes=65_000_000

time: 61.7 us -> 56.4 us (0.914)
  Pallas kernels: 59.4 us -> 54.5 us
    pallas_call x1, Pallas kernels: 58.4 us -> 53.5 us  [on_device(): pl.pallas_call(kernel, name='patch_attention', out_shape=(V((1, 128, 1024...]
where the time goes in v4:
time: 56.4 us; the launch traced here: 55.8 us
  Pallas kernels  54.5 us (97%)
  between operations  1.29 us (2%)
    pallas_call x1, Pallas kernels, on_device(): pl.pallas_call(kernel, name='patch_attention', out_shape=(V((1, 128, 1024...  53.5 us

profile of v4, /device:TPU:6, one launch (start us, length us, event | category | flops | bytes accessed | tf_op | source)
XLA Modules:
  0.0 55.8 jit_solution(1849783805191186991)
XLA Ops:
  1.3 53.5 %patch_attention.1 = (bf16[1,128,1024]{2,1,0:T(8,128)(2,1)S(1)}, bf16[1,128,1024]{2,1,0:T(8,128)(2,1)S(1)}, bf16[1,128,1024]{2,1,0:T(8,128)(2,1)S(1)}, bf16[1,128,1024]{2,1,0:T(8,128)(2,1)S(1)}, f32[2,1024]{1,0:T(2,128)S(1)}) custom-call(s32[1,1,2]{2,1,0:T(1,128)} %nbr_h.1, s32[1,1]{1,0:T(1,128)S(6)} %copy.12.cnt, bf16[1,128,1024]{2,1,0:T(8,128)(2,1)} %q_h.1, ...), custom_call_target="tpu_custom_call" | custom-call | tf_op jit(solution)/shard_map/patch_attention/pallas_call | solution.py:331
  54.8 1.0 %flush.1 = (bf16[1,128,1024]{2,1,0:T(8,128)(2,1)}, bf16[1,128,1024]{2,1,0:T(8,128)(2,1)}, bf16[1,128,1024]{2,1,0:T(8,128)(2,1)}, bf16[1,128,1024]{2,1,0:T(8,128)(2,1)}, f32[2,1024]{1,0:T(2,128)}) custom-call(bf16[1,128,1024]{2,1,0:T(8,128)(2,1)S(1)} %get-tuple-element.10.refs_0_, bf16[1,128,1024]{2,1,0:T(8,128)(2,1)S(1)} %get-tuple-element.11.refs_1_, ...), custom_call_target="tpu_custom_call" | custom-call | tf_op jit(solution)/shard_map/flush/pallas_call | solution.py:362

commit v5 on v4

--- a/solution.py
+++ b/solution.py
@@ -277,8 +277,6 @@
             send(cot.at[xr], cot.at[xr], cs.at[4, 1], cr.at[4, 1], grp(partner))
 
     pass_parts(1)
-    a_all = att[...]
-    out_r[0] = sum(dot(a_all[:, i * PW:(i + 1) * PW], w[i], 1, 0) for i in range(PAIRS)).astype(BF)
     pass_parts(2)
     cot_wait(partner, None, 2, 0)
     cot_wait(flip(xl), None, 4, 0)
@@ -286,6 +284,8 @@
     cot_wait(flip(xo), None, 2, 1)
     pl.semaphore_wait(far, NY - 1)
     reduce_rows(0, 4)
+    a_all = att[...]
+    out_r[0] = sum(dot(a_all[:, i * PW:(i + 1) * PW], w[i], 1, 0) for i in range(PAIRS)).astype(BF)
     pass_parts(3)
 
     for i in range(PAIRS):

time: 56.4 us -> 56.4 us (level)
  no operation moved by 1% of the time
where the time goes in v5:
time: 56.4 us; the launch traced here: 55.8 us
  Pallas kernels  54.5 us (97%)
  between operations  1.29 us (2%)
    pallas_call x1, Pallas kernels, on_device(): pl.pallas_call(kernel, name='patch_attention', out_shape=(V((1, 128, 1024...  53.5 us

profile of v5, /device:TPU:6, one launch (start us, length us, event | category | flops | bytes accessed | tf_op | source)
XLA Modules:
  0.0 55.8 jit_solution(7356280824467303408)
XLA Ops:
  1.3 53.5 %patch_attention.1 = (bf16[1,128,1024]{2,1,0:T(8,128)(2,1)S(1)}, bf16[1,128,1024]{2,1,0:T(8,128)(2,1)S(1)}, bf16[1,128,1024]{2,1,0:T(8,128)(2,1)S(1)}, bf16[1,128,1024]{2,1,0:T(8,128)(2,1)S(1)}, f32[2,1024]{1,0:T(2,128)S(1)}) custom-call(s32[1,1,2]{2,1,0:T(1,128)} %nbr_h.1, s32[1,1]{1,0:T(1,128)S(6)} %copy.12.cnt, bf16[1,128,1024]{2,1,0:T(8,128)(2,1)} %q_h.1, ...), custom_call_target="tpu_custom_call" | custom-call | tf_op jit(solution)/shard_map/patch_attention/pallas_call | solution.py:331
  54.8 1.0 %flush.1 = (bf16[1,128,1024]{2,1,0:T(8,128)(2,1)}, bf16[1,128,1024]{2,1,0:T(8,128)(2,1)}, bf16[1,128,1024]{2,1,0:T(8,128)(2,1)}, bf16[1,128,1024]{2,1,0:T(8,128)(2,1)}, f32[2,1024]{1,0:T(2,128)}) custom-call(bf16[1,128,1024]{2,1,0:T(8,128)(2,1)S(1)} %get-tuple-element.10.refs_0_, bf16[1,128,1024]{2,1,0:T(8,128)(2,1)S(1)} %get-tuple-element.11.refs_1_, ...), custom_call_target="tpu_custom_call" | custom-call | tf_op jit(solution)/shard_map/flush/pallas_call | solution.py:362

commit v6 on v5

--- a/solution.py
+++ b/solution.py
@@ -193,7 +193,9 @@
         zs[pl.ds(first * 16, count)] = term.reshape(count, 16, 128).astype(BF)
 
         def hand_out(k, carry):
-            c = first * 16 + (me + k) % count
+            t = k // NY
+            dz = 4 + ((t + 1) // 2) * (1 - 2 * (t % 2))
+            c = ((z + dz) % NZ) * NY + (y + 4 + k) % NY
 
             @pl.when(c != me)
             def _():

time: 56.4 us -> 55.8 us (0.989)
  no operation moved by 1% of the time
where the time goes in v6:
time: 55.8 us; the launch traced here: 55.7 us
  Pallas kernels  54.4 us (97%)
  between operations  1.29 us (2%)
    pallas_call x1, Pallas kernels, on_device(): pl.pallas_call(kernel, name='patch_attention', out_shape=(V((1, 128, 1024...  53.4 us

profile of v6, /device:TPU:6, one launch (start us, length us, event | category | flops | bytes accessed | tf_op | source)
XLA Modules:
  0.0 55.7 jit_solution(13141523444113875881)
XLA Ops:
  1.3 53.4 %patch_attention.1 = (bf16[1,128,1024]{2,1,0:T(8,128)(2,1)S(1)}, bf16[1,128,1024]{2,1,0:T(8,128)(2,1)S(1)}, bf16[1,128,1024]{2,1,0:T(8,128)(2,1)S(1)}, bf16[1,128,1024]{2,1,0:T(8,128)(2,1)S(1)}, f32[2,1024]{1,0:T(2,128)S(1)}) custom-call(s32[1,1,2]{2,1,0:T(1,128)} %nbr_h.1, s32[1,1]{1,0:T(1,128)S(6)} %copy.12.cnt, bf16[1,128,1024]{2,1,0:T(8,128)(2,1)} %q_h.1, ...), custom_call_target="tpu_custom_call" | custom-call | tf_op jit(solution)/shard_map/patch_attention/pallas_call | solution.py:333
  54.7 1.0 %flush.1 = (bf16[1,128,1024]{2,1,0:T(8,128)(2,1)}, bf16[1,128,1024]{2,1,0:T(8,128)(2,1)}, bf16[1,128,1024]{2,1,0:T(8,128)(2,1)}, bf16[1,128,1024]{2,1,0:T(8,128)(2,1)}, f32[2,1024]{1,0:T(2,128)}) custom-call(bf16[1,128,1024]{2,1,0:T(8,128)(2,1)S(1)} %get-tuple-element.10.refs_0_, bf16[1,128,1024]{2,1,0:T(8,128)(2,1)S(1)} %get-tuple-element.11.refs_1_, ...), custom_call_target="tpu_custom_call" | custom-call | tf_op jit(solution)/shard_map/flush/pallas_call | solution.py:364
